TPU v7x, 256 devices: a whole 4x4x8 slice. The times are simulated.
256 devices in a mesh: subcube: 2 (over y_hi), row: 8 (over z), col: 16 (over x, y_lo, core).
Axes of the slice: x: 4, y: 4 (y_hi: 2, y_lo: 2; y = y_hi * 2 + y_lo), z: 8, core: 2. Of those that a mesh axis runs over, the one named last changes fastest.
Arguments:
- front_entries: float32 [16, 8, 64, 24576], P('col', 'row', None, 'subcube'), may hold values from -6 to 6
- child_blocks: float32 [2, 16, 8, 64, 12288], P('subcube', 'col', 'row'), may hold values from -6 to 6
- row_maps: int32 [2, 12288], replicated, may hold values from 0 to 24575, as said below
- pivot_inverses: float32 [2, 512, 512], P(None, 'row')
- tile_mask: int32 [48, 16], P(('subcube', 'row'), 'col'), may hold values 0 or 1
Outputs:
- factored: float32 [24576, 8192], P(('subcube', 'row'), 'col')
Inputs may be any that keep to these rules, and one draw needn't show every extreme that they name: Each row of row_maps lists 12288 distinct front rows in increasing order; its first is 0 and its last 24575.
All inputs are finite; a program needn't handle non-finite values. No bound on the sum of `tile_mask` on one device may be relied on, other than what follows from the above.
Results may differ from a plain program's by a relative error of at most 0.0001.
Values sent between devices are 32-bit elements; how exact they have to be, the bound alone decides.
No kernel may reach another device: no remote copies, remote signals or barrier semaphores. Data moves between devices by JAX's collectives and lax.ppermute only.
A program may use at most 128 MiB of HBM per device.

v0:
```python
import jax
import jax.numpy as jnp
from jax import lax
from jax.sharding import PartitionSpec as P

PANEL = 512
PANELS = 2


def broadcast(value, axis, source):
    kept = jnp.where(lax.axis_index(axis) == source, value, 0).astype(value.dtype)
    return lax.psum(kept, axis)


def from_partner(x, axis, distance):
    return lax.ppermute(x, axis, [(i, i ^ 1 << distance) for i in range(lax.axis_size(axis))])


def product(left, right):
    return jnp.dot(left, right, precision=lax.Precision.HIGHEST, preferred_element_type=jnp.float32)


def extend_add(target, child_rows, row_map, offset):
    local_rows = row_map - offset
    inside = (local_rows >= 0) & (local_rows < target.shape[1])
    target_rows = jnp.where(inside, local_rows, target.shape[1])
    return target.at[:, target_rows].add(child_rows, mode="drop")


def send_strip(row_strip, root_row):
    return broadcast(row_strip, ("subcube", "row"), root_row)


def local(front_entries, child_blocks, row_maps, pivot_inverses, tile_mask):
    half_rows = front_entries.shape[3]
    subcube_side = lax.axis_index("subcube")
    own_block = child_blocks[0, 0, 0]
    partner_block = from_partner(own_block, "subcube", 0)
    own_map = lax.dynamic_index_in_dim(row_maps, subcube_side, 0, keepdims=False)
    partner_map = lax.dynamic_index_in_dim(row_maps, 1 - subcube_side, 0, keepdims=False)
    assembled = front_entries[0, 0]
    assembled = extend_add(assembled, own_block, own_map, subcube_side * half_rows)
    assembled = extend_add(assembled, partner_block, partner_map, subcube_side * half_rows)
    regrouped = lax.all_to_all(assembled, "row", split_axis=1, concat_axis=0, tiled=True)
    local_block = regrouped.T
    row_count = local_block.shape[0]
    block_width = local_block.shape[1]
    column_place = lax.axis_index("col")
    column_ids = column_place * block_width + jnp.arange(block_width, dtype=jnp.int32)
    grid_row = subcube_side * lax.axis_size("row") + lax.axis_index("row")
    row_ids = grid_row * row_count + jnp.arange(row_count, dtype=jnp.int32)
    kept_tiles = jnp.repeat(jnp.repeat(tile_mask.astype(jnp.float32), PANEL, axis=0), PANEL, axis=1)
    for panel_index in range(PANELS):
        first_col = panel_index * PANEL
        after_col = first_col + PANEL
        owner_col = first_col // block_width
        local_start = first_col - owner_col * block_width
        root_row = first_col // row_count
        row_start = first_col - root_row * row_count
        panel_cols = local_block
        row_strip = local_block[row_start : row_start + PANEL, :]
        inverse = lax.all_gather(pivot_inverses[panel_index], "row", axis=0, tiled=True)
        scaled = broadcast(product(panel_cols, inverse), "col", owner_col)
        across = send_strip(row_strip, root_row)
        update = product(scaled, across)
        below = (row_ids >= after_col).astype(jnp.float32)[:, None]
        live_mask = kept_tiles * (column_ids >= after_col).astype(jnp.float32)[None, :] * below
        local_block = local_block - update * live_mask
        current = local_block
        replace = (column_place == owner_col) & (row_ids >= first_col)[:, None]
        local_block = local_block.at[:, local_start : local_start + PANEL].set(
            jnp.where(replace, scaled, current)
        )
    return local_block


def solution(mesh):
    return jax.shard_map(
        local,
        mesh=mesh,
        in_specs=(
            P("col", "row", None, "subcube"),
            P("subcube", "col", "row", None, None),
            P(),
            P(None, "row", None),
            P(("subcube", "row"), "col"),
        ),
        out_specs=P(("subcube", "row"), "col"),
        check_vma=False,
    )
```

profile of v0, /device:TPU:1, one launch (start us, length us, event | category | flops | bytes accessed | tf_op | source)
XLA Modules:
  0.0 864.5 jit_solution(14957715034153878558)
XLA Ops:
  7.4 3.7 collective-permute-start
  11.1 0.0 copy-start
  11.1 5.9 copy.10
  17.0 0.0 copy-done
  17.0 0.0 copy-start.2
  17.0 4.0 copy.11
  21.0 0.0 copy-done.2
  21.0 0.3 compare_select_fusion
  21.3 64.7 %scatter_fusion = f32[64,12288]{0,1:T(8,128)} fusion(f32[64,12288]{0,1:T(8,128)} %bitcast.31, s32[12288]{0:T(1024)S(1)} %bitcast.39, f32[12288,64]{1,0:T(8,128)} %copy.11), kind=kCustom, calls=%fused_computation | custom fusion | flops 786432 | bytes 9486336 | tf_op jit(solution)/shard_map/scatter-add | solution.py:27
  86.1 0.0 collective-permute-done
  86.1 5.8 copy.12
  91.8 64.7 %scatter_fusion.1 = f32[64,12288]{0,1:T(8,128)} fusion(f32[64,12288]{0,1:T(8,128)} %scatter_fusion, s32[12288]{0:T(1024)S(1)} %bitcast.38, f32[12288,64]{1,0:T(8,128)} %copy.12), kind=kCustom, calls=%fused_computation.1 | custom fusion | flops 786432 | bytes 9486336 | tf_op jit(solution)/shard_map/scatter-add | solution.py:27
  156.6 6.1 copy.13
  162.7 0.0 copy-start.1
  162.7 8.3 all-to-all-start
  171.0 0.0 all-gather.5.cloned.1.call-start
  171.0 0.0 copy-done.1
  171.0 0.7 fusion.17
  171.8 0.0 all-gather.5.cloned.1.call-update
  171.8 0.0 all-reduce.7.cloned.1.call-start
  171.8 81.7 %all-to-all-done = f32[64,8,1536]{2,0,1:T(8,128)S(1)} async-done(((f32[64,8,1536]{2,0,1:T(8,128)}), f32[64,8,1536]{2,0,1:T(8,128)S(1)}, u32[]{:S(2)}, u32[]{:S(2)}) %all-to-all-start) | async-done | bytes 3145760 | tf_op jit(solution)/shard_map/all_to_all | solution.py:44
  253.6 2.3 copy.14
  255.9 2.4 slice_select_fusion.1
  258.3 0.0 all-reduce.7.cloned.1.call-update
  258.3 0.2 all-reduce.5.cloned.1.call-start
  258.6 0.0 all-gather.5.cloned.1.call-done
  258.6 12.4 %convolution_select_fusion.1 = f32[1536,512]{1,0:T(8,128)} fusion(f32[512,1536]{1,0:T(8,128)S(1)} %bitcast.34, pred[]{:T(512)S(6)} %eq.13, f32[1,512,512]{2,1,0:T(8,128)} %all-gather.5.cloned.1.call-done), kind=kOutput, calls=%fused_computation.3 | convolution fusion | flops 4832624640 | bytes 7340033 | tf_op jit(solution)/shard_map/dot_general | solution.py:20
  271.0 0.0 copy-start.3
  271.0 0.0 all-reduce.5.cloned.1.call-update
  271.0 0.0 all-gather.7.cloned.1.call-start
  271.0 0.7 all-gather.7.cloned.1.call-update
  271.8 0.0 all-reduce.11.cloned.1.call-start
  271.8 0.0 copy-done.3
  271.8 0.1 broadcast_in_dim.44
  271.9 130.9 %all-reduce.7.cloned.1.call-done = f32[512,512]{1,0:T(8,128)} async-done(((f32[512,512]{1,0:T(8,128)}), f32[512,512]{1,0:T(8,128)}) %all-reduce.7.cloned.1.call-update) | async-done | bytes 1048592 | tf_op jit(solution)/shard_map/psum | solution.py:12
  402.8 142.3 %all-reduce.5.cloned.1.call-done = f32[1536,512]{1,0:T(8,128)} async-done(((f32[1536,512]{1,0:T(8,128)}), f32[1536,512]{1,0:T(8,128)}) %all-reduce.5.cloned.1.call-update) | async-done | bytes 3145744 | tf_op jit(solution)/shard_map/psum | solution.py:12
  545.1 9.6 %fusion.1 = f32[1536,512]{1,0:T(8,128)S(1)} fusion(f32[1536,512]{1,0:T(8,128)} %all-reduce.5.cloned.1.call-done, f32[512,512]{1,0:T(8,128)} %all-reduce.7.cloned.1.call-done, f32[1536]{0:T(1024)S(1)} %get-tuple-element.49, f32[512]{0:T(512)S(1)} %fusion.15, f32[1536]{0:T(1024)S(1)} %broadcast_in_dim.45, pred[1536]{0:T(1024)(128)(4,1)S(1)} %get-tuple-element.50, ...), kind=kOutput, calls=%fused_computation.7 | convolution fusion | flops 4835770368 | bytes 10501632 | tf_op jit(solution)/shard_map/dot_general | solution.py:20
  554.7 1.1 slice_select_fusion
  555.8 0.0 all-reduce.11.cloned.1.call-update
  555.8 0.3 all-reduce.9.cloned.1.call-start
  556.1 0.0 all-gather.7.cloned.1.call-done
  556.1 7.5 convolution_select_fusion
  563.6 0.0 all-reduce.9.cloned.1.call-update
  563.6 141.0 %all-reduce.11.cloned.1.call-done = f32[512,512]{1,0:T(8,128)} async-done(((f32[512,512]{1,0:T(8,128)}), f32[512,512]{1,0:T(8,128)}) %all-reduce.11.cloned.1.call-update) | async-done | bytes 1048592 | tf_op jit(solution)/shard_map/psum | solution.py:12
  704.6 142.5 %all-reduce.9.cloned.1.call-done = f32[1536,512]{1,0:T(8,128)} async-done(((f32[1536,512]{1,0:T(8,128)}), f32[1536,512]{1,0:T(8,128)}) %all-reduce.9.cloned.1.call-update) | async-done | bytes 3145744 | tf_op jit(solution)/shard_map/psum | solution.py:12
  847.1 9.9 %fusion.3 = f32[1536,512]{1,0:T(8,128)} fusion(f32[1536,512]{1,0:T(8,128)} %all-reduce.9.cloned.1.call-done, f32[1536,512]{1,0:T(8,128)S(1)} %fusion.1, f32[512,512]{1,0:T(8,128)} %all-reduce.11.cloned.1.call-done, f32[1536]{0:T(1024)S(1)} %get-tuple-element.52, f32[512]{0:T(512)S(1)} %fusion.16, f32[1536]{0:T(1024)S(1)} %broadcast_in_dim.45, ...), kind=kOutput, calls=%fused_computation.9 | convolution fusion | flops 4835770368 | bytes 10501632 | tf_op jit(solution)/shard_map/dot_general | solution.py:20
  (6 shorter events, 0.0 us)
Async XLA Ops:
  7.4 78.7 %collective-permute-start = (f32[64,12288]{1,0:T(8,128)}, f32[64,12288]{1,0:T(8,128)}, u32[]{:S(2)}, u32[]{:S(2)}) collective-permute-start(f32[64,12288]{1,0:T(8,128)} %bitcast.36), channel_id=1, source_target_pairs={{0,128},{128,0},{1,129},{129,1},{2,130},{130,2},{3,131},{131,3},{4... | collective-permute-start | bytes 9437192 | tf_op jit(solution)/shard_map/ppermute | solution.py:16
  11.1 5.9 copy-start
  17.0 4.0 copy-start.2
  162.7 8.4 copy-start.1
  162.7 90.9 %all-to-all-start = ((f32[64,8,1536]{2,0,1:T(8,128)}), f32[64,8,1536]{2,0,1:T(8,128)S(1)}, u32[]{:S(2)}, u32[]{:S(2)}) async-start(f32[64,8,1536]{2,0,1:T(8,128)} %copy.13), calls=%async_computation | async-start | bytes 6291456 | tf_op jit(solution)/shard_map/all_to_all | solution.py:44
  171.0 87.6 %all-gather.5.cloned.1.call-start = ((), (), s32[]{:S(2)}) async-start(), calls=%async_computation.5 | async-start | bytes 1179648 | tf_op jit(solution)/shard_map/all_gather | solution.py:62
  171.8 231.0 %all-reduce.7.cloned.1.call-start = ((), (), s32[]{:S(2)}) async-start(), calls=%async_computation.2 | async-start | bytes 2097152 | tf_op jit(solution)/shard_map/psum | solution.py:12
  258.3 286.8 %all-reduce.5.cloned.1.call-start = ((), (), s32[]{:S(2)}) async-start(), calls=%async_computation.1 | async-start | bytes 6291456 | tf_op jit(solution)/shard_map/psum | solution.py:12
  271.0 0.8 copy-start.3
  271.0 285.1 %all-gather.7.cloned.1.call-start = ((), (), s32[]{:S(2)}) async-start(), calls=%async_computation.6 | async-start | bytes 1179648 | tf_op jit(solution)/shard_map/all_gather | solution.py:62
  271.8 432.8 %all-reduce.11.cloned.1.call-start = ((), (), s32[]{:S(2)}) async-start(), calls=%async_computation.4 | async-start | bytes 2097152 | tf_op jit(solution)/shard_map/psum | solution.py:12
  555.8 291.3 %all-reduce.9.cloned.1.call-start = ((), (), s32[]{:S(2)}) async-start(), calls=%async_computation.3 | async-start | bytes 6291456 | tf_op jit(solution)/shard_map/psum | solution.py:12
Sparse Core Ops, SparseCore 0:
  173.7 55.4 all-gather.4
  273.6 30.5 all-gather.6
Sparse Core Ops, SparseCore 1:
  258.4 144.4 all-reduce.6
  405.6 139.5 all-reduce.4
  555.9 148.6 all-reduce.10
  707.3 139.7 all-reduce.8
where the time goes:
time: 865 us
  waiting for transfers between devices  639 us (74%)
  other arithmetic  133 us (15%)
  matrix products  39.3 us (5%)
  local copies, waits for them, and re-layouts  24.9 us (3%)
  between operations  15.2 us (2%)
  starting transfers between devices  12.7 us (1%)
    psum x4, waiting for transfers between devices, broadcast(): return lax.psum(kept, axis)  557 us
    scatter-add x2, other arithmetic, extend_add(): return target.at[:, target_rows].add(child_rows, mode='drop')  129 us
    all_to_all x1, waiting for transfers between devices, local(): lax.all_to_all(assembled, 'row', split_axis=1, concat_axis=0, tiled=True)  81.7 us
    dot_general x4, matrix products, product(): jnp.dot(left, right, precision=lax.Precision.HIGHEST, preferred_element_t...  39.3 us
  transfers between devices with their start and end apart: 8, of which 5 were waited for; matrix products, arithmetic and copies ran while one was open for 13% of the time, Pallas kernels for 0%

commit v1 on v0

--- a/solution.py
+++ b/solution.py
@@ -41,7 +41,10 @@
     assembled = front_entries[0, 0]
     assembled = extend_add(assembled, own_block, own_map, subcube_side * half_rows)
     assembled = extend_add(assembled, partner_block, partner_map, subcube_side * half_rows)
-    regrouped = lax.all_to_all(assembled, "row", split_axis=1, concat_axis=0, tiled=True)
+    regrouped = jnp.concatenate(
+        lax.all_to_all(jnp.stack(jnp.split(assembled, lax.axis_size("row"), axis=1)), "row", 0, 0),
+        axis=0,
+    )
     local_block = regrouped.T
     row_count = local_block.shape[0]
     block_width = local_block.shape[1]

time: 865 us -> 882 us (1.020)
  local copies, waits for them, and re-layouts: 24.9 us -> 41.5 us
    unnamed x9 -> x16, local copies, waits for them, and re-layouts: 5.92 us -> 20.4 us
where the time goes in v1:
time: 882 us; the launch traced here: 881 us
  waiting for transfers between devices  639 us (72%)
  other arithmetic  133 us (15%)
  local copies, waits for them, and re-layouts  41.5 us (5%)
  matrix products  39.3 us (4%)
  between operations  15.2 us (2%)
  starting transfers between devices  12.7 us (1%)
    psum x4, waiting for transfers between devices, broadcast(): return lax.psum(kept, axis)  557 us
    scatter-add x2, other arithmetic, extend_add(): return target.at[:, target_rows].add(child_rows, mode='drop')  129 us
    all_to_all x1, waiting for transfers between devices, local(): lax.all_to_all(jnp.stack(jnp.split(assembled, lax.axis_size('row'), axis=...  81.7 us
    dot_general x4, matrix products, product(): jnp.dot(left, right, precision=lax.Precision.HIGHEST, preferred_element_t...  39.3 us
    unnamed x16, local copies, waits for them, and re-layouts  20.4 us
  transfers between devices with their start and end apart: 8, of which 5 were waited for; matrix products, arithmetic and copies ran while one was open for 13% of the time, Pallas kernels for 0%

profile of v1, /device:TPU:1, one launch (start us, length us, event | category | flops | bytes accessed | tf_op | source)
XLA Modules:
  0.0 881.1 jit_solution(17679707837251174198)
XLA Ops:
  7.4 3.7 collective-permute-start
  11.1 5.9 copy.15
  17.0 0.0 copy-done
  17.0 4.0 copy.16
  21.0 0.0 copy-done.2
  21.0 0.3 compare_select_fusion
  21.3 64.7 %scatter_fusion = f32[64,12288]{0,1:T(8,128)} fusion(f32[64,12288]{0,1:T(8,128)} %bitcast.60, s32[12288]{0:T(1024)S(1)} %bitcast.67, f32[12288,64]{1,0:T(8,128)} %copy.16), kind=kCustom, calls=%fused_computation | custom fusion | flops 786432 | bytes 9486336 | tf_op jit(solution)/shard_map/scatter-add | solution.py:27
  86.1 0.0 collective-permute-done
  86.1 5.8 copy.17
  91.8 64.7 %scatter_fusion.1 = f32[64,12288]{0,1:T(8,128)} fusion(f32[64,12288]{0,1:T(8,128)} %scatter_fusion, s32[12288]{0:T(1024)S(1)} %bitcast.66, f32[12288,64]{1,0:T(8,128)} %copy.17), kind=kCustom, calls=%fused_computation.1 | custom fusion | flops 786432 | bytes 9486336 | tf_op jit(solution)/shard_map/scatter-add | solution.py:27
  156.6 2.1 fusion.13
  158.6 2.1 fusion.12
  160.7 2.0 fusion.11
  162.8 2.1 fusion.10
  164.8 2.1 fusion.9
  166.9 2.1 fusion.8
  169.0 2.1 fusion.7
  171.1 2.1 fusion.6
  173.1 6.1 copy.18
  179.3 8.3 all-to-all-start
  187.6 0.0 all-gather.5.cloned.1.call-start
  187.6 0.7 fusion.25
  188.3 0.0 all-gather.5.cloned.1.call-update
  188.4 0.0 all-reduce.7.cloned.1.call-start
  188.4 81.7 %all-to-all-done = f32[8,64,1536]{2,1,0:T(8,128)S(1)} async-done(((f32[8,64,1536]{2,1,0:T(8,128)}), f32[8,64,1536]{2,1,0:T(8,128)S(1)}, u32[]{:S(2)}, u32[]{:S(2)}) %all-to-all-start) | async-done | bytes 3145760 | tf_op jit(solution)/shard_map/all_to_all | solution.py:45
  270.2 2.3 copy.19
  272.5 2.4 slice_select_fusion.1
  274.9 0.0 all-reduce.7.cloned.1.call-update
  274.9 0.2 all-reduce.5.cloned.1.call-start
  275.1 0.0 all-gather.5.cloned.1.call-done
  275.2 12.4 %convolution_select_fusion.1 = f32[1536,512]{1,0:T(8,128)} fusion(f32[512,1536]{1,0:T(8,128)S(1)} %bitcast.62, pred[]{:T(512)S(6)} %eq.13, f32[1,512,512]{2,1,0:T(8,128)} %all-gather.5.cloned.1.call-done), kind=kOutput, calls=%fused_computation.3 | convolution fusion | flops 4832624640 | bytes 7340033 | tf_op jit(solution)/shard_map/dot_general | solution.py:20
  287.6 0.0 all-reduce.5.cloned.1.call-update
  287.6 0.0 all-gather.7.cloned.1.call-start
  287.6 0.7 all-gather.7.cloned.1.call-update
  288.3 0.0 all-reduce.11.cloned.1.call-start
  288.4 0.1 broadcast_in_dim.44
  288.5 130.9 %all-reduce.7.cloned.1.call-done = f32[512,512]{1,0:T(8,128)} async-done(((f32[512,512]{1,0:T(8,128)}), f32[512,512]{1,0:T(8,128)}) %all-reduce.7.cloned.1.call-update) | async-done | bytes 1048592 | tf_op jit(solution)/shard_map/psum | solution.py:12
  419.4 142.3 %all-reduce.5.cloned.1.call-done = f32[1536,512]{1,0:T(8,128)} async-done(((f32[1536,512]{1,0:T(8,128)}), f32[1536,512]{1,0:T(8,128)}) %all-reduce.5.cloned.1.call-update) | async-done | bytes 3145744 | tf_op jit(solution)/shard_map/psum | solution.py:12
  561.7 9.6 %fusion.1 = f32[1536,512]{1,0:T(8,128)S(1)} fusion(f32[1536,512]{1,0:T(8,128)} %all-reduce.5.cloned.1.call-done, f32[512,512]{1,0:T(8,128)} %all-reduce.7.cloned.1.call-done, f32[1536]{0:T(1024)S(1)} %get-tuple-element.49, f32[512]{0:T(512)S(1)} %fusion.23, f32[1536]{0:T(1024)S(1)} %broadcast_in_dim.45, pred[1536]{0:T(1024)(128)(4,1)S(1)} %get-tuple-element.50, ...), kind=kOutput, calls=%fused_computation.7 | convolution fusion | flops 4835770368 | bytes 10501632 | tf_op jit(solution)/shard_map/dot_general | solution.py:20
  571.3 1.1 slice_select_fusion
  572.4 0.0 all-reduce.11.cloned.1.call-update
  572.4 0.3 all-reduce.9.cloned.1.call-start
  572.7 0.0 all-gather.7.cloned.1.call-done
  572.7 7.5 convolution_select_fusion
  580.1 0.0 all-reduce.9.cloned.1.call-update
  580.2 141.0 %all-reduce.11.cloned.1.call-done = f32[512,512]{1,0:T(8,128)} async-done(((f32[512,512]{1,0:T(8,128)}), f32[512,512]{1,0:T(8,128)}) %all-reduce.11.cloned.1.call-update) | async-done | bytes 1048592 | tf_op jit(solution)/shard_map/psum | solution.py:12
  721.2 142.5 %all-reduce.9.cloned.1.call-done = f32[1536,512]{1,0:T(8,128)} async-done(((f32[1536,512]{1,0:T(8,128)}), f32[1536,512]{1,0:T(8,128)}) %all-reduce.9.cloned.1.call-update) | async-done | bytes 3145744 | tf_op jit(solution)/shard_map/psum | solution.py:12
  863.6 9.9 %fusion.3 = f32[1536,512]{1,0:T(8,128)} fusion(f32[1536,512]{1,0:T(8,128)} %all-reduce.9.cloned.1.call-done, f32[1536,512]{1,0:T(8,128)S(1)} %fusion.1, f32[512,512]{1,0:T(8,128)} %all-reduce.11.cloned.1.call-done, f32[1536]{0:T(1024)S(1)} %get-tuple-element.52, f32[512]{0:T(512)S(1)} %fusion.24, f32[1536]{0:T(1024)S(1)} %broadcast_in_dim.45, ...), kind=kOutput, calls=%fused_computation.9 | convolution fusion | flops 4835770368 | bytes 10501632 | tf_op jit(solution)/shard_map/dot_general | solution.py:20
  (12 shorter events, 0.1 us)
Async XLA Ops:
  7.4 78.7 %collective-permute-start = (f32[64,12288]{1,0:T(8,128)}, f32[64,12288]{1,0:T(8,128)}, u32[]{:S(2)}, u32[]{:S(2)}) collective-permute-start(f32[64,12288]{1,0:T(8,128)} %bitcast.64), channel_id=1, source_target_pairs={{0,128},{128,0},{1,129},{129,1},{2,130},{130,2},{3,131},{131,3},{4... | collective-permute-start | bytes 9437192 | tf_op jit(solution)/shard_map/ppermute | solution.py:16
  11.1 5.9 copy-start
  17.0 4.0 copy-start.2
  179.3 8.4 copy-start.1
  179.3 90.9 %all-to-all-start = ((f32[8,64,1536]{2,1,0:T(8,128)}), f32[8,64,1536]{2,1,0:T(8,128)S(1)}, u32[]{:S(2)}, u32[]{:S(2)}) async-start(f32[8,64,1536]{2,1,0:T(8,128)} %copy.18), calls=%async_computation | async-start | bytes 6291456 | tf_op jit(solution)/shard_map/all_to_all | solution.py:45
  187.6 87.6 %all-gather.5.cloned.1.call-start = ((), (), s32[]{:S(2)}) async-start(), calls=%async_computation.5 | async-start | bytes 1179648 | tf_op jit(solution)/shard_map/all_gather | solution.py:65
  188.4 231.0 %all-reduce.7.cloned.1.call-start = ((), (), s32[]{:S(2)}) async-start(), calls=%async_computation.2 | async-start | bytes 2097152 | tf_op jit(solution)/shard_map/psum | solution.py:12
  274.9 286.8 %all-reduce.5.cloned.1.call-start = ((), (), s32[]{:S(2)}) async-start(), calls=%async_computation.1 | async-start | bytes 6291456 | tf_op jit(solution)/shard_map/psum | solution.py:12
  287.6 0.8 copy-start.3
  287.6 285.1 %all-gather.7.cloned.1.call-start = ((), (), s32[]{:S(2)}) async-start(), calls=%async_computation.6 | async-start | bytes 1179648 | tf_op jit(solution)/shard_map/all_gather | solution.py:65
  288.3 432.8 %all-reduce.11.cloned.1.call-start = ((), (), s32[]{:S(2)}) async-start(), calls=%async_computation.4 | async-start | bytes 2097152 | tf_op jit(solution)/shard_map/psum | solution.py:12
  572.4 291.3 %all-reduce.9.cloned.1.call-start = ((), (), s32[]{:S(2)}) async-start(), calls=%async_computation.3 | async-start | bytes 6291456 | tf_op jit(solution)/shard_map/psum | solution.py:12
Sparse Core Ops, SparseCore 0:
  190.3 55.4 all-gather.4
  290.2 30.5 all-gather.6
Sparse Core Ops, SparseCore 1:
  275.0 144.4 all-reduce.6
  422.1 139.5 all-reduce.4
  572.5 148.6 all-reduce.10
  723.9 139.7 all-reduce.8
